TPU v7x, 32 devices: a whole 2x2x4 slice. The times are simulated.
32 devices in a mesh: pipe: 2 (over x), expert: 16 (over z, y, core).
Axes of the slice: x: 2, y: 2, z: 4, core: 2. Of those that a mesh axis runs over, the one named last changes fastest.
Arguments:
- inputs: bfloat16 [1, 512, 5120], P(None, 'expert'), may hold values from -6 to 6
- router: bfloat16 [2, 5120, 2], P('pipe'), may hold values from -0.078125 to 0.078125
- w_up: bfloat16 [2, 3072, 5120], P('pipe', 'expert'), may hold values from -0.078125 to 0.078125
- w_down: bfloat16 [2, 3072, 5120], P('pipe', 'expert'), may hold values from -0.15625 to 0.15625
- picks: int32 [2, 1, 2, 8], P('pipe'), may hold values from 0 to 511, as said below
- probe: bfloat16 [2, 64, 5120], P('pipe'), may hold values from -0.078125 to 0.078125
Outputs:
- student_feats: bfloat16 [2, 1, 512, 64], P('pipe', None, 'expert')
Inputs may be any that keep to these rules, and one draw needn't show every extreme that they name: Each list picks[s, m, e] holds 8 different token positions of the micro-batch. Of the 32 consecutive positions held by one index of expert, at most 1 stand in one list, and in every list some index has exactly 1.
All inputs are finite; a program needn't handle non-finite values.
Results may differ from a plain program's by a relative error of at most 0.0059.
Values may be sent and summed in bfloat16 or wider, within the bound.
A program may use at most 64 MiB of HBM per device.

v0:
```python
import jax
import jax.numpy as jnp
from jax import lax
from jax.sharding import PartitionSpec as P

SLOT = 1


def passed_along(x, axis, by):
    size = lax.axis_size(axis)
    pairs = [(i, i + by) for i in range(size) if 0 <= i + by < size]
    return lax.ppermute(x, axis, pairs)


def from_root(x, axis, root):
    mine = lax.axis_index(axis) == root
    return lax.psum(jnp.where(mine, x, jnp.zeros_like(x)), axis)


def rms_rows(rows_in):
    wide = rows_in.astype(jnp.float32)
    scale = lax.rsqrt(jnp.mean(wide * wide, axis=-1, keepdims=True) + 1e-06)
    return (wide * scale).astype(jnp.bfloat16)


def shards(inputs, router, w_up, w_down, picks, probe):
    sections = lax.axis_size("pipe")
    expert_width = lax.axis_size("expert")
    section_index = lax.axis_index("pipe")
    source = lax.axis_index("expert")
    micro_count, tok_rows, features = inputs.shape
    experts = router.shape[2]
    group_size = expert_width // experts
    tick_count = micro_count + sections - 1
    positions = jnp.arange(tok_rows, dtype=jnp.int32)
    slot_ids = jnp.arange(SLOT, dtype=jnp.int32)

    def expert_rows(received):
        row_shape = received.shape
        flat_rows = received.reshape(-1, row_shape[2])
        pre = lax.dot_general(
            flat_rows, w_up[0], (((1,), (1,)), ((), ())), preferred_element_type=jnp.float32
        )
        hidden = jax.nn.silu(pre).astype(jnp.bfloat16)
        partials = jnp.dot(hidden, w_down[0], preferred_element_type=jnp.float32).astype(
            jnp.bfloat16
        )
        return partials.reshape(row_shape)

    def layer(rows_in, micro_index):
        normed = rms_rows(rows_in)
        gate_values = jax.nn.sigmoid(jnp.dot(normed, router[0], preferred_element_type=jnp.float32))
        chosen = lax.dynamic_index_in_dim(picks[0], micro_index, 0, keepdims=False)
        local_rows = chosen - source * tok_rows
        owned = (local_rows >= 0) & (local_rows < tok_rows)
        owned_count = owned.astype(jnp.int32)
        slot_place = jnp.cumsum(owned_count, axis=1) - owned_count
        slot_hot = ((slot_place[:, :, None] == slot_ids) & owned[:, :, None]).astype(jnp.bfloat16)
        row_hot = (local_rows[:, :, None] == positions).astype(jnp.bfloat16)
        selector = jnp.einsum("ecr,ect->ert", slot_hot, row_hot, preferred_element_type=jnp.float32)
        picked = jnp.einsum(
            "ert,td->erd", selector.astype(jnp.bfloat16), normed, preferred_element_type=jnp.float32
        ).astype(jnp.bfloat16)
        copies = jnp.repeat(picked, group_size, axis=0)
        partials = expert_rows(
            lax.all_to_all(copies, "expert", split_axis=0, concat_axis=0, tiled=True)
        )
        returned = lax.all_to_all(partials, "expert", split_axis=0, concat_axis=0, tiled=True)
        expert_out = jnp.sum(
            returned.astype(jnp.float32).reshape(experts, group_size, SLOT, features), axis=1
        )
        weights = selector * jnp.transpose(gate_values)[:, None, :]
        update = jnp.einsum("ert,erd->td", weights, expert_out, precision=lax.Precision.HIGHEST)
        return (rows_in.astype(jnp.float32) + update).astype(jnp.bfloat16)

    def tick(tick_index, loop_state):
        previous, finals = loop_state
        arrived = passed_along(previous, "pipe", 1)
        micro_index = jnp.clip(tick_index - section_index, 0, micro_count - 1)
        fresh_rows = lax.dynamic_index_in_dim(
            inputs, jnp.clip(tick_index, 0, micro_count - 1), 0, keepdims=False
        )
        rows_in = jnp.where(section_index == 0, fresh_rows, arrived)
        result = layer(rows_in, micro_index)
        finished = (
            (section_index == sections - 1)
            & (tick_index - section_index >= 0)
            & (tick_index - section_index < micro_count)
        )
        stored = lax.dynamic_update_index_in_dim(finals, result, micro_index, 0)
        finals = jnp.where(finished, stored, finals)
        return (result, finals)

    start_rows = jnp.zeros((tok_rows, features), jnp.bfloat16)
    start_finals = jnp.zeros((micro_count, tok_rows, features), jnp.bfloat16)
    previous, finals = lax.fori_loop(0, tick_count, tick, (start_rows, start_finals))
    shared = from_root(finals, "pipe", sections - 1)
    final_normed = rms_rows(shared)
    student_rows = jnp.einsum(
        "mtd,jd->mtj", final_normed, probe[0], preferred_element_type=jnp.float32
    )
    return student_rows.astype(jnp.bfloat16)[None]


def solution(mesh):
    return jax.shard_map(
        shards,
        mesh=mesh,
        in_specs=(
            P(None, "expert", None),
            P("pipe", None, None),
            P("pipe", "expert", None),
            P("pipe", "expert", None),
            P("pipe", None, None, None),
            P("pipe", None, None),
        ),
        out_specs=P("pipe", None, "expert", None),
        check_vma=False,
    )
```

profile of v0, /device:TPU:0, one launch (start us, length us, event | category | flops | bytes accessed | tf_op | source)
XLA Modules:
  0.0 138.6 jit_solution(14568044816781589299)
XLA Ops:
  6.5 0.7 fusion.38
  7.3 0.2 reduce_window_sum.19
  7.5 0.2 fusion.35
  7.7 95.9 %while.21 = (s32[]{:T(128)}, bf16[32,5120]{1,0:T(8,128)(2,1)}, bf16[1,32,5120]{2,1,0:T(8,128)(2,1)}, pred[]{:T(512)}, bf16[1,32,5120]{2,1,0:T(8,128)(2,1)}, /*in...) while((s32[]{:T(128)}, bf16[32,5120]{1,0:T(8,128)(2,1)}, ...), condition=%wide.region_4.5_spmd.clone, body=%wide.region_1.4_spmd.clone.sunk | while | flops 71040296 | bytes 23656336 | solution.py:96
  7.7 5.0 %collective-permute-start = (bf16[32,5120]{1,0:T(8,128)(2,1)S(1)}, bf16[32,5120]{1,0:T(8,128)(2,1)S(1)}, u32[]{:S(2)}, u32[]{:S(2)}) collective-permute-start(bf16[32,5120]{1,0:T(8,128)(2,1)S(1)} %broadcast_select_fusion.3), channel_id=1, source_target_pairs={{0,16},{1,17},{2,18},{3,19},{4,20},{5,21},{6,22},{7,23},{8,24},{9,... | collective-permute-start | bytes 983048 | tf_op jit(solution)/shard_map/while/body/eval_jaxpr/ppermute | solution.py:12
  12.7 6.9 %collective-permute-done = bf16[32,5120]{1,0:T(8,128)(2,1)S(1)} collective-permute-done((bf16[32,5120]{1,0:T(8,128)(2,1)S(1)}, bf16[32,5120]{1,0:T(8,128)(2,1)S(1)}, u32[]{:S(2)}, u32[]{:S(2)}) %collective-permute-start) | collective-permute-done | bytes 327712 | tf_op jit(solution)/shard_map/while/body/eval_jaxpr/ppermute | solution.py:12
  19.7 1.2 fusion.64
  20.9 0.2 fusion.65
  21.2 0.6 broadcast.199
  21.8 0.8 reduce.13
  22.6 14.2 %all_to_all.32 = bf16[16,2,2560]{2,1,0:T(2,128)(2,1)S(1)} all-to-all(bf16[16,2,2560]{2,1,0:T(2,128)(2,1)S(1)} %reshape.138), channel_id=1, replica_groups=mesh['pipe'=2,'expert'=16] {'expert'}, dimensions={0} | all-to-all | bytes 327680 | tf_op jit(solution)/shard_map/while/body/eval_jaxpr/all_to_all | solution.py:66
  36.8 0.1 reshape.139
  37.0 3.0 %fusion.66 = bf16[16,1,5120]{2,0,1:T(8,128)(2,1)S(1)} fusion(bf16[1,192,5120]{2,1,0:T(8,128)(2,1)} %get-tuple-element.587, bf16[1,192,5120]{2,1,0:T(8,128)(2,1)S(1)} %copy-done.1, bf16[16,1,5120]{2,1,0:T(2,128)(2,1)S(1)} %reshape.139), kind=kOutput, calls=%fused_computation.3.clone.1 | convolution fusion | flops 63011840 | bytes 4259840 | tf_op jit(solution)/shard_map/while/body/eval_jaxpr/dot_general | solution.py:45
  40.0 0.6 broadcast.200
  40.6 0.8 reduce.14
  41.4 0.8 reshape.140
  42.1 3.5 %all-to-all-start.1 = ((bf16[16,2,2560]{2,1,0:T(2,128)(2,1)}), bf16[16,2,2560]{2,1,0:T(2,128)(2,1)S(1)}, u32[]{:S(2)}, u32[]{:S(2)}) async-start(bf16[16,2,2560]{2,1,0:T(2,128)(2,1)} %reshape.140), calls=%async_computation.1 | async-start | bytes 327680 | tf_op jit(solution)/shard_map/while/body/eval_jaxpr/all_to_all | solution.py:68
  45.7 0.3 fusion.67
  45.9 8.1 %all-to-all-done.1 = bf16[16,2,2560]{2,1,0:T(2,128)(2,1)S(1)} async-done(((bf16[16,2,2560]{2,1,0:T(2,128)(2,1)}), bf16[16,2,2560]{2,1,0:T(2,128)(2,1)S(1)}, u32[]{:S(2)}, u32[]{:S(2)}) %all-to-all-start.1) | async-done | bytes 163872 | tf_op jit(solution)/shard_map/while/body/eval_jaxpr/all_to_all | solution.py:68
  54.0 0.1 reshape.141
  54.2 0.3 reshape.142
  54.5 0.1 bitcast_reduce_fusion.2
  54.7 1.6 %bitcast_select_fusion.4 = (bf16[1,32,5120]{2,1,0:T(8,128)(2,1)S(1)}, bf16[32,5120]{1,0:T(8,128)(2,1)}) fusion(bf16[1,32,5120]{2,1,0:T(8,128)(2,1)S(1)} %copy-done.2, pred[]{:T(512)S(6)} %compare.3, pred[]{:T(512)S(6)} %and.69, f32[2,32]{1,0:T(2,128)S(1)} %fusion.67, f32[2,5120]{1,0:T(2,128)S(1)} %bitcast_reduce_fusion.2, ...), kind=kOutput, calls=%fused_computation.20.clone.1 | convolution fusion | flops 4751360 | bytes 1351938 | tf_op jit(solution)/shard_map/while/body/eval_jaxpr/ert,erd->td/dot_general | solution.py:73
  56.2 0.7 copy-done.3
  57.0 1.1 broadcast_select_fusion.3
  58.1 4.4 %collective-permute-start = (bf16[32,5120]{1,0:T(8,128)(2,1)S(1)}, bf16[32,5120]{1,0:T(8,128)(2,1)S(1)}, u32[]{:S(2)}, u32[]{:S(2)}) collective-permute-start(bf16[32,5120]{1,0:T(8,128)(2,1)S(1)} %broadcast_select_fusion.3), channel_id=1, source_target_pairs={{0,16},{1,17},{2,18},{3,19},{4,20},{5,21},{6,22},{7,23},{8,24},{9,... | collective-permute-start | bytes 983048 | tf_op jit(solution)/shard_map/while/body/eval_jaxpr/ppermute | solution.py:12
  62.5 6.3 %collective-permute-done = bf16[32,5120]{1,0:T(8,128)(2,1)S(1)} collective-permute-done((bf16[32,5120]{1,0:T(8,128)(2,1)S(1)}, bf16[32,5120]{1,0:T(8,128)(2,1)S(1)}, u32[]{:S(2)}, u32[]{:S(2)}) %collective-permute-start) | collective-permute-done | bytes 327712 | tf_op jit(solution)/shard_map/while/body/eval_jaxpr/ppermute | solution.py:12
  68.9 1.2 fusion.64
  70.1 0.2 fusion.65
  70.4 0.6 broadcast.199
  71.0 0.8 reduce.13
  71.8 11.6 %all_to_all.32 = bf16[16,2,2560]{2,1,0:T(2,128)(2,1)S(1)} all-to-all(bf16[16,2,2560]{2,1,0:T(2,128)(2,1)S(1)} %reshape.138), channel_id=1, replica_groups=mesh['pipe'=2,'expert'=16] {'expert'}, dimensions={0} | all-to-all | bytes 327680 | tf_op jit(solution)/shard_map/while/body/eval_jaxpr/all_to_all | solution.py:66
  83.6 3.0 %fusion.66 = bf16[16,1,5120]{2,0,1:T(8,128)(2,1)S(1)} fusion(bf16[1,192,5120]{2,1,0:T(8,128)(2,1)} %get-tuple-element.587, bf16[1,192,5120]{2,1,0:T(8,128)(2,1)S(1)} %copy-done.1, bf16[16,1,5120]{2,1,0:T(2,128)(2,1)S(1)} %reshape.139), kind=kOutput, calls=%fused_computation.3.clone.1 | convolution fusion | flops 63011840 | bytes 4259840 | tf_op jit(solution)/shard_map/while/body/eval_jaxpr/dot_general | solution.py:45
  86.6 0.6 broadcast.200
  87.2 0.8 reduce.14
  88.0 0.8 reshape.140
  88.7 3.5 %all-to-all-start.1 = ((bf16[16,2,2560]{2,1,0:T(2,128)(2,1)}), bf16[16,2,2560]{2,1,0:T(2,128)(2,1)S(1)}, u32[]{:S(2)}, u32[]{:S(2)}) async-start(bf16[16,2,2560]{2,1,0:T(2,128)(2,1)} %reshape.140), calls=%async_computation.1 | async-start | bytes 327680 | tf_op jit(solution)/shard_map/while/body/eval_jaxpr/all_to_all | solution.py:68
  92.3 0.3 fusion.67
  92.6 8.1 %all-to-all-done.1 = bf16[16,2,2560]{2,1,0:T(2,128)(2,1)S(1)} async-done(((bf16[16,2,2560]{2,1,0:T(2,128)(2,1)}), bf16[16,2,2560]{2,1,0:T(2,128)(2,1)S(1)}, u32[]{:S(2)}, u32[]{:S(2)}) %all-to-all-start.1) | async-done | bytes 163872 | tf_op jit(solution)/shard_map/while/body/eval_jaxpr/all_to_all | solution.py:68
  100.7 0.1 reshape.141
  100.8 0.3 reshape.142
  101.1 0.1 bitcast_reduce_fusion.2
  101.3 1.6 %bitcast_select_fusion.4 = (bf16[1,32,5120]{2,1,0:T(8,128)(2,1)S(1)}, bf16[32,5120]{1,0:T(8,128)(2,1)}) fusion(bf16[1,32,5120]{2,1,0:T(8,128)(2,1)S(1)} %copy-done.2, pred[]{:T(512)S(6)} %compare.3, pred[]{:T(512)S(6)} %and.69, f32[2,32]{1,0:T(2,128)S(1)} %fusion.67, f32[2,5120]{1,0:T(2,128)S(1)} %bitcast_reduce_fusion.2, ...), kind=kOutput, calls=%fused_computation.20.clone.1 | convolution fusion | flops 4751360 | bytes 1351938 | tf_op jit(solution)/shard_map/while/body/eval_jaxpr/ert,erd->td/dot_general | solution.py:73
  102.9 0.7 copy-done.3
  103.6 0.7 broadcast_select_fusion.1
  104.4 24.3 %all-reduce.2.cloned.1.call-done = bf16[1,32,5120]{2,1,0:T(8,128)(2,1)} async-done(((bf16[1,32,5120]{2,1,0:T(8,128)(2,1)}), bf16[1,32,5120]{2,1,0:T(8,128)(2,1)}) %all-reduce.2.cloned.1.call-update) | async-done | bytes 327696 | tf_op jit(solution)/shard_map/psum | solution.py:17
  128.6 1.1 fusion.29
  129.8 1.9 %fusion.28 = bf16[1,1,32,64]{3,2,1,0:T(8,128)(2,1)} fusion(bf16[1,64,5120]{2,1,0:T(8,128)(2,1)S(1)} %copy-done, bf16[1,32,5120]{2,1,0:T(8,128)(2,1)} %all-reduce.2.cloned.1.call-done, f32[32]{0:T(128)S(1)} %add_rsqrt_fusion.1), kind=kOutput, calls=%fused_computation.32 | convolution fusion | flops 21465088 | bytes 987264 | tf_op jit(solution)/shard_map/mtd,jd->mtj/dot_general | solution.py:99
  (31 shorter events, 0.5 us)
Async XLA Ops:
  6.5 123.3 %copy-start = (bf16[1,64,5120]{2,1,0:T(8,128)(2,1)S(1)}, bf16[1,64,5120]{2,1,0:T(8,128)(2,1)}, u32[]{:S(2)}) copy-start(bf16[1,64,5120]{2,1,0:T(8,128)(2,1)} %param.13) | copy-start | bytes 1966084
  6.5 122.1 %all-reduce.2.cloned.1.call-start = ((), (), s32[]{:S(2)}) async-start(), calls=%async_computation.2 | async-start | bytes 655360 | tf_op jit(solution)/shard_map/psum | solution.py:17
  7.7 29.3 %copy-start.1 = (bf16[1,192,5120]{2,1,0:T(8,128)(2,1)S(1)}, bf16[1,192,5120]{2,1,0:T(8,128)(2,1)}, u32[]{:S(2)}) copy-start(bf16[1,192,5120]{2,1,0:T(8,128)(2,1)} %get-tuple-element.586) | copy-start | bytes 5898244 | tf_op jit(solution)/shard_map/while
  7.7 12.0 %collective-permute-start = (bf16[32,5120]{1,0:T(8,128)(2,1)S(1)}, bf16[32,5120]{1,0:T(8,128)(2,1)S(1)}, u32[]{:S(2)}, u32[]{:S(2)}) collective-permute-start(bf16[32,5120]{1,0:T(8,128)(2,1)S(1)} %broadcast_select_fusion.3), channel_id=1, source_target_pairs={{0,16},{1,17},{2,18},{3,19},{4,20},{5,21},{6,22},{7,23},{8,24},{9,... | collective-permute-start | bytes 983048 | tf_op jit(solution)/shard_map/while/body/eval_jaxpr/ppermute | solution.py:12
  36.9 8.7 %copy-start.4 = (bf16[1,5120,2]{1,2,0:T(2,128)(2,1)S(1)}, bf16[1,5120,2]{1,2,0:T(2,128)(2,1)}, u32[]{:S(2)}) copy-start(bf16[1,5120,2]{1,2,0:T(2,128)(2,1)} %get-tuple-element.583) | copy-start | bytes 61444 | tf_op jit(solution)/shard_map/while
  40.0 14.7 %copy-start.2 = (bf16[1,32,5120]{2,1,0:T(8,128)(2,1)S(1)}, bf16[1,32,5120]{2,1,0:T(8,128)(2,1)}, u32[]{:S(2)}) copy-start(bf16[1,32,5120]{2,1,0:T(8,128)(2,1)} %get-tuple-element.564) | copy-start | bytes 983044 | tf_op jit(solution)/shard_map/while
  42.1 11.9 %all-to-all-start.1 = ((bf16[16,2,2560]{2,1,0:T(2,128)(2,1)}), bf16[16,2,2560]{2,1,0:T(2,128)(2,1)S(1)}, u32[]{:S(2)}, u32[]{:S(2)}) async-start(bf16[16,2,2560]{2,1,0:T(2,128)(2,1)} %reshape.140), calls=%async_computation.1 | async-start | bytes 327680 | tf_op jit(solution)/shard_map/while/body/eval_jaxpr/all_to_all | solution.py:68
  56.2 0.7 copy-start.3
  57.0 26.6 %copy-start.1 = (bf16[1,192,5120]{2,1,0:T(8,128)(2,1)S(1)}, bf16[1,192,5120]{2,1,0:T(8,128)(2,1)}, u32[]{:S(2)}) copy-start(bf16[1,192,5120]{2,1,0:T(8,128)(2,1)} %get-tuple-element.586) | copy-start | bytes 5898244 | tf_op jit(solution)/shard_map/while
  58.1 10.8 %collective-permute-start = (bf16[32,5120]{1,0:T(8,128)(2,1)S(1)}, bf16[32,5120]{1,0:T(8,128)(2,1)S(1)}, u32[]{:S(2)}, u32[]{:S(2)}) collective-permute-start(bf16[32,5120]{1,0:T(8,128)(2,1)S(1)} %broadcast_select_fusion.3), channel_id=1, source_target_pairs={{0,16},{1,17},{2,18},{3,19},{4,20},{5,21},{6,22},{7,23},{8,24},{9,... | collective-permute-start | bytes 983048 | tf_op jit(solution)/shard_map/while/body/eval_jaxpr/ppermute | solution.py:12
  83.6 8.7 %copy-start.4 = (bf16[1,5120,2]{1,2,0:T(2,128)(2,1)S(1)}, bf16[1,5120,2]{1,2,0:T(2,128)(2,1)}, u32[]{:S(2)}) copy-start(bf16[1,5120,2]{1,2,0:T(2,128)(2,1)} %get-tuple-element.583) | copy-start | bytes 61444 | tf_op jit(solution)/shard_map/while
  86.6 14.7 %copy-start.2 = (bf16[1,32,5120]{2,1,0:T(8,128)(2,1)S(1)}, bf16[1,32,5120]{2,1,0:T(8,128)(2,1)}, u32[]{:S(2)}) copy-start(bf16[1,32,5120]{2,1,0:T(8,128)(2,1)} %get-tuple-element.564) | copy-start | bytes 983044 | tf_op jit(solution)/shard_map/while
  88.7 11.9 %all-to-all-start.1 = ((bf16[16,2,2560]{2,1,0:T(2,128)(2,1)}), bf16[16,2,2560]{2,1,0:T(2,128)(2,1)S(1)}, u32[]{:S(2)}, u32[]{:S(2)}) async-start(bf16[16,2,2560]{2,1,0:T(2,128)(2,1)} %reshape.140), calls=%async_computation.1 | async-start | bytes 327680 | tf_op jit(solution)/shard_map/while/body/eval_jaxpr/all_to_all | solution.py:68
  102.9 0.7 copy-start.3
Sparse Core Ops, SparseCore 0:
  104.5 24.1 all-reduce.1
where the time goes:
time: 139 us
  waiting for transfers between devices  53.8 us (39%)
  blocking collectives  25.8 us (19%)
  starting transfers between devices  16.5 us (12%)
  between operations  13.4 us (10%)
  matrix products  12.4 us (9%)
  other arithmetic  10.4 us (7%)
  local copies, waits for them, and re-layouts  6.15 us (4%)
    all_to_all x2, blocking collectives, layer(): lax.all_to_all(copies, 'expert', split_axis=0, concat_axis=0, tiled=True)  25.8 us
    psum x1, waiting for transfers between devices, from_root(): return lax.psum(jnp.where(mine, x, jnp.zeros_like(x)), axis)  24.3 us
    all_to_all x2, waiting for transfers between devices, layer(): lax.all_to_all(partials, 'expert', split_axis=0, concat_axis=0, tiled=True)  16.2 us
    ppermute x2, waiting for transfers between devices, passed_along(): return lax.ppermute(x, axis, pairs)  13.3 us
    ppermute x2, starting transfers between devices, passed_along(): return lax.ppermute(x, axis, pairs)  9.43 us
    all_to_all x2, starting transfers between devices, layer(): lax.all_to_all(partials, 'expert', split_axis=0, concat_axis=0, tiled=True)  7.03 us
    dot_general x2, matrix products, expert_rows(): jnp.dot(hidden, w_down[0], preferred_element_type=jnp.float32)  6.05 us
    while x24, local copies, waits for them, and re-layouts  3.7 us
  transfers between devices with their start and end apart: 5, of which 5 were waited for; matrix products, arithmetic and copies ran while one was open for 0% of the time, Pallas kernels for 0%

commit v1 on v0

--- a/solution.py
+++ b/solution.py
@@ -4,6 +4,25 @@
 from jax.sharding import PartitionSpec as P
 
 SLOT = 1
+
+
+def floor_treat(frame_in):
+    step_out, state_next = (lax.psum(1, axis_name="expert"), lax.axis_index("expert"))
+    top = frame_in.shape[0] // step_out
+    tall = list(frame_in.shape)
+    tall[0] = top
+    frame_out = tall[0]
+    tall[0] = frame_out * step_out
+    val2 = jnp.zeros(tall, frame_in.dtype)
+    for u in range(step_out):
+        t1 = lax.dynamic_slice_in_dim(frame_in, (state_next ^ u) * top, top, axis=0)
+        if u:
+            kept_rows = []
+            for m in range(step_out):
+                kept_rows.append((m, m ^ u))
+            t1 = lax.ppermute(t1, axis_name="expert", perm=kept_rows)
+        val2 = lax.dynamic_update_slice_in_dim(val2, t1, (state_next ^ u) * frame_out, axis=0)
+    return val2
 
 
 def passed_along(x, axis, by):
@@ -62,9 +81,7 @@
             "ert,td->erd", selector.astype(jnp.bfloat16), normed, preferred_element_type=jnp.float32
         ).astype(jnp.bfloat16)
         copies = jnp.repeat(picked, group_size, axis=0)
-        partials = expert_rows(
-            lax.all_to_all(copies, "expert", split_axis=0, concat_axis=0, tiled=True)
-        )
+        partials = expert_rows(floor_treat(copies))
         returned = lax.all_to_all(partials, "expert", split_axis=0, concat_axis=0, tiled=True)
         expert_out = jnp.sum(
             returned.astype(jnp.float32).reshape(experts, group_size, SLOT, features), axis=1

time: 139 us -> 161 us (1.16)
  starting transfers between devices: 16.5 us -> 58.7 us
  blocking collectives: 25.8 us -> 0 us
  local copies, waits for them, and re-layouts: 6.15 us -> 14.2 us
  other arithmetic: 10.4 us -> 7.52 us
    ppermute x0 -> x30, starting transfers between devices: none -> 41.2 us  [floor_treat(): t1 = lax.ppermute(t1, axis_name='expert', perm=kept_rows)]
    all_to_all x2 -> x0, blocking collectives: 25.8 us -> none  [layer(): lax.all_to_all(copies, 'expert', split_axis=0, concat_axis=0, tiled=True)]
    dynamic_update_slice x0 -> x32, local copies, waits for them, and re-layouts: none -> 9.1 us  [floor_treat(): lax.dynamic_update_slice_in_dim(val2, t1, (state_next ^ u) * frame_out, a...]
    while x24 -> x20, local copies, waits for them, and re-layouts: 3.7 us -> 3.23 us
  transfers between devices with their start and end apart: 5 -> 35, of which waited for: 5 -> 6; matrix products, arithmetic and copies ran while one was open for 0% -> 6% of each run, Pallas kernels for 0% -> 0%
where the time goes in v1:
time: 161 us
  starting transfers between devices  58.7 us (36%)
  waiting for transfers between devices  55 us (34%)
  local copies, waits for them, and re-layouts  14.2 us (9%)
  between operations  13.4 us (8%)
  matrix products  11 us (7%)
  other arithmetic  7.52 us (5%)
    ppermute x30, starting transfers between devices, floor_treat(): t1 = lax.ppermute(t1, axis_name='expert', perm=kept_rows)  41.2 us
    psum x1, waiting for transfers between devices, from_root(): return lax.psum(jnp.where(mine, x, jnp.zeros_like(x)), axis)  24.3 us
    all_to_all x2, waiting for transfers between devices, layer(): lax.all_to_all(partials, 'expert', split_axis=0, concat_axis=0, tiled=True)  16.2 us
    ppermute x2, waiting for transfers between devices, passed_along(): return lax.ppermute(x, axis, pairs)  13.1 us
    ppermute x2, starting transfers between devices, passed_along(): return lax.ppermute(x, axis, pairs)  9.56 us
    dynamic_update_slice x32, local copies, waits for them, and re-layouts, floor_treat(): lax.dynamic_update_slice_in_dim(val2, t1, (state_next ^ u) * frame_out, a...  9.1 us
    all_to_all x2, starting transfers between devices, layer(): lax.all_to_all(partials, 'expert', split_axis=0, concat_axis=0, tiled=True)  8.02 us
    dot_general x2, matrix products, expert_rows(): jnp.dot(hidden, w_down[0], preferred_element_type=jnp.float32)  6.06 us
  transfers between devices with their start and end apart: 35, of which 6 were waited for; matrix products, arithmetic and copies ran while one was open for 6% of the time, Pallas kernels for 0%

profile of v1, /device:TPU:0, one launch (start us, length us, event | category | flops | bytes accessed | tf_op | source)
XLA Modules:
  0.0 160.7 jit_solution(10407103792041353097)
XLA Ops:
  6.5 0.7 fusion.32
  7.7 118.0 %while.21 = (s32[]{:T(128)}, bf16[32,5120]{1,0:T(8,128)(2,1)S(1)}, bf16[1,32,5120]{2,1,0:T(8,128)(2,1)}, pred[]{:T(512)}, bf16[1,32,5120]{2,1,0:T(8,128)(2,1)}, ...) while((s32[]{:T(128)}, bf16[32,5120]{1,0:T(8,128)(2,1)S(1)}, ...), condition=%wide.region_4.5_spmd.clone, body=%wide.region_1.4_spmd.clone.sunk | while | flops 71040360 | bytes 23944652 | solution.py:113
  7.7 5.0 %collective-permute-start = (bf16[32,5120]{1,0:T(8,128)(2,1)S(1)}, bf16[32,5120]{1,0:T(8,128)(2,1)S(1)}, u32[]{:S(2)}, u32[]{:S(2)}) collective-permute-start(bf16[32,5120]{1,0:T(8,128)(2,1)S(1)} %broadcast_select_fusion.3), channel_id=1, source_target_pairs={{0,16},{1,17},{2,18},{3,19},{4,20},{5,21},{6,22},{7,23},{8,24},{9,... | collective-permute-start | bytes 983048 | tf_op jit(solution)/shard_map/while/body/eval_jaxpr/ppermute | solution.py:31
  12.8 6.8 %collective-permute-done = bf16[32,5120]{1,0:T(8,128)(2,1)S(1)} collective-permute-done((bf16[32,5120]{1,0:T(8,128)(2,1)S(1)}, bf16[32,5120]{1,0:T(8,128)(2,1)S(1)}, u32[]{:S(2)}, u32[]{:S(2)}) %collective-permute-start) | collective-permute-done | bytes 327712 | tf_op jit(solution)/shard_map/while/body/eval_jaxpr/ppermute | solution.py:31
  19.7 1.2 fusion.59
  21.6 1.6 collective-permute-start.2
  23.5 1.6 collective-permute-start.4
  25.2 2.5 %collective-permute-start.6 = (bf16[1,1,5120]{2,0,1:T(2,128)(2,1)S(1)}, bf16[1,1,5120]{2,0,1:T(2,128)(2,1)S(1)}, u32[]{:S(2)}, u32[]{:S(2)}) collective-permute-start(bf16[1,1,5120]{2,0,1:T(2,128)(2,1)S(1)} %get-tuple-element.585), channel_id=1, source_target_pairs={{0,6},{1,7},{2,4},{3,5},{4,2},{5,3},{6,0},{7,1},{8,14},{9,15},{10,... | collective-permute-start | bytes 30728 | tf_op jit(solution)/shard_map/while/body/eval_jaxpr/ppermute | solution.py:23
  27.9 2.6 %collective-permute-start.8 = (bf16[1,1,5120]{2,0,1:T(2,128)(2,1)S(1)}, bf16[1,1,5120]{2,0,1:T(2,128)(2,1)S(1)}, u32[]{:S(2)}, u32[]{:S(2)}) collective-permute-start(bf16[1,1,5120]{2,0,1:T(2,128)(2,1)S(1)} %get-tuple-element.587), channel_id=1, source_target_pairs={{0,8},{1,9},{2,10},{3,11},{4,12},{5,13},{6,14},{7,15},{8,0},{9,1},... | collective-permute-start | bytes 30728 | tf_op jit(solution)/shard_map/while/body/eval_jaxpr/ppermute | solution.py:23
  30.6 3.5 %collective-permute-start.10 = (bf16[1,1,5120]{2,0,1:T(2,128)(2,1)S(1)}, bf16[1,1,5120]{2,0,1:T(2,128)(2,1)S(1)}, u32[]{:S(2)}, u32[]{:S(2)}) collective-permute-start(bf16[1,1,5120]{2,0,1:T(2,128)(2,1)S(1)} %get-tuple-element.589), channel_id=1, source_target_pairs={{0,10},{1,11},{2,8},{3,9},{4,14},{5,15},{6,12},{7,13},{8,2},{9,3},... | collective-permute-start | bytes 30728 | tf_op jit(solution)/shard_map/while/body/eval_jaxpr/ppermute | solution.py:23
  34.2 3.5 %collective-permute-start.12 = (bf16[1,1,5120]{2,0,1:T(2,128)(2,1)S(1)}, bf16[1,1,5120]{2,0,1:T(2,128)(2,1)S(1)}, u32[]{:S(2)}, u32[]{:S(2)}) collective-permute-start(bf16[1,1,5120]{2,0,1:T(2,128)(2,1)S(1)} %get-tuple-element.591), channel_id=1, source_target_pairs={{0,12},{1,13},{2,14},{3,15},{4,8},{5,9},{6,10},{7,11},{8,4},{9,5},... | collective-permute-start | bytes 30728 | tf_op jit(solution)/shard_map/while/body/eval_jaxpr/ppermute | solution.py:23
  37.7 4.4 %collective-permute-start.14 = (bf16[1,1,5120]{2,0,1:T(2,128)(2,1)S(1)}, bf16[1,1,5120]{2,0,1:T(2,128)(2,1)S(1)}, u32[]{:S(2)}, u32[]{:S(2)}) collective-permute-start(bf16[1,1,5120]{2,0,1:T(2,128)(2,1)S(1)} %get-tuple-element.593), channel_id=1, source_target_pairs={{0,14},{1,15},{2,12},{3,13},{4,10},{5,11},{6,8},{7,9},{8,6},{9,7},... | collective-permute-start | bytes 30728 | tf_op jit(solution)/shard_map/while/body/eval_jaxpr/ppermute | solution.py:23
  46.8 1.3 collective-permute-done.15
  48.4 3.0 %fusion.61 = bf16[16,1,5120]{2,0,1:T(8,128)(2,1)S(1)} fusion(bf16[1,192,5120]{2,1,0:T(8,128)(2,1)} %get-tuple-element.670, bf16[16,5120]{1,0:T(8,128)(2,1)S(1)} %dynamic_update_slice.259, bf16[1,192,5120]{2,1,0:T(8,128)(2,1)S(1)} %copy-done.1), kind=kOutput, calls=%fused_computation.3.clone.1 | convolution fusion | flops 63011840 | bytes 4259840 | tf_op jit(solution)/shard_map/while/body/eval_jaxpr/dot_general | solution.py:64
  51.9 0.6 reduce.11
  52.5 0.8 reshape.326
  53.3 4.5 %all-to-all-start = ((bf16[16,2,2560]{2,1,0:T(2,128)(2,1)}), bf16[16,2,2560]{2,1,0:T(2,128)(2,1)S(1)}, u32[]{:S(2)}, u32[]{:S(2)}) async-start(bf16[16,2,2560]{2,1,0:T(2,128)(2,1)} %reshape.326), calls=%async_computation | async-start | bytes 327680 | tf_op jit(solution)/shard_map/while/body/eval_jaxpr/all_to_all | solution.py:85
  58.1 8.1 %all-to-all-done = bf16[16,2,2560]{2,1,0:T(2,128)(2,1)S(1)} async-done(((bf16[16,2,2560]{2,1,0:T(2,128)(2,1)}), bf16[16,2,2560]{2,1,0:T(2,128)(2,1)S(1)}, u32[]{:S(2)}, u32[]{:S(2)}) %all-to-all-start) | async-done | bytes 163872 | tf_op jit(solution)/shard_map/while/body/eval_jaxpr/all_to_all | solution.py:85
  66.8 0.9 bitcast_select_fusion.4
  67.7 0.7 copy-done.3
  68.5 4.5 %collective-permute-start = (bf16[32,5120]{1,0:T(8,128)(2,1)S(1)}, bf16[32,5120]{1,0:T(8,128)(2,1)S(1)}, u32[]{:S(2)}, u32[]{:S(2)}) collective-permute-start(bf16[32,5120]{1,0:T(8,128)(2,1)S(1)} %broadcast_select_fusion.3), channel_id=1, source_target_pairs={{0,16},{1,17},{2,18},{3,19},{4,20},{5,21},{6,22},{7,23},{8,24},{9,... | collective-permute-start | bytes 983048 | tf_op jit(solution)/shard_map/while/body/eval_jaxpr/ppermute | solution.py:31
  73.1 6.3 %collective-permute-done = bf16[32,5120]{1,0:T(8,128)(2,1)S(1)} collective-permute-done((bf16[32,5120]{1,0:T(8,128)(2,1)S(1)}, bf16[32,5120]{1,0:T(8,128)(2,1)S(1)}, u32[]{:S(2)}, u32[]{:S(2)}) %collective-permute-start) | collective-permute-done | bytes 327712 | tf_op jit(solution)/shard_map/while/body/eval_jaxpr/ppermute | solution.py:31
  79.4 1.2 fusion.59
  81.3 0.8 collective-permute-start.2
  82.1 1.1 collective-permute-start.3
  83.2 0.9 collective-permute-start.4
  84.1 0.8 collective-permute-start.5
  84.9 1.1 collective-permute-start.6
  86.0 1.6 collective-permute-start.7
  87.6 1.0 collective-permute-start.8
  88.5 1.6 %collective-permute-start.9 = (bf16[1,1,5120]{2,0,1:T(2,128)(2,1)S(1)}, bf16[1,1,5120]{2,0,1:T(2,128)(2,1)S(1)}, u32[]{:S(2)}, u32[]{:S(2)}) collective-permute-start(bf16[1,1,5120]{2,0,1:T(2,128)(2,1)S(1)} %get-tuple-element.588), channel_id=1, source_target_pairs={{0,9},{1,8},{2,11},{3,10},{4,13},{5,12},{6,15},{7,14},{8,1},{9,0},... | collective-permute-start | bytes 30728 | tf_op jit(solution)/shard_map/while/body/eval_jaxpr/ppermute | solution.py:23
  90.2 1.1 collective-permute-start.10
  91.3 2.4 %collective-permute-start.11 = (bf16[1,1,5120]{2,0,1:T(2,128)(2,1)S(1)}, bf16[1,1,5120]{2,0,1:T(2,128)(2,1)S(1)}, u32[]{:S(2)}, u32[]{:S(2)}) collective-permute-start(bf16[1,1,5120]{2,0,1:T(2,128)(2,1)S(1)} %get-tuple-element.590), channel_id=1, source_target_pairs={{0,11},{1,10},{2,9},{3,8},{4,15},{5,14},{6,13},{7,12},{8,3},{9,2},... | collective-permute-start | bytes 30728 | tf_op jit(solution)/shard_map/while/body/eval_jaxpr/ppermute | solution.py:23
  93.8 1.8 %collective-permute-start.12 = (bf16[1,1,5120]{2,0,1:T(2,128)(2,1)S(1)}, bf16[1,1,5120]{2,0,1:T(2,128)(2,1)S(1)}, u32[]{:S(2)}, u32[]{:S(2)}) collective-permute-start(bf16[1,1,5120]{2,0,1:T(2,128)(2,1)S(1)} %get-tuple-element.591), channel_id=1, source_target_pairs={{0,12},{1,13},{2,14},{3,15},{4,8},{5,9},{6,10},{7,11},{8,4},{9,5},... | collective-permute-start | bytes 30728 | tf_op jit(solution)/shard_map/while/body/eval_jaxpr/ppermute | solution.py:23
  95.6 1.7 %collective-permute-start.13 = (bf16[1,1,5120]{2,0,1:T(2,128)(2,1)S(1)}, bf16[1,1,5120]{2,0,1:T(2,128)(2,1)S(1)}, u32[]{:S(2)}, u32[]{:S(2)}) collective-permute-start(bf16[1,1,5120]{2,0,1:T(2,128)(2,1)S(1)} %get-tuple-element.592), channel_id=1, source_target_pairs={{0,13},{1,12},{2,15},{3,14},{4,9},{5,8},{6,11},{7,10},{8,5},{9,4},... | collective-permute-start | bytes 30728 | tf_op jit(solution)/shard_map/while/body/eval_jaxpr/ppermute | solution.py:23
  97.3 2.0 %collective-permute-start.14 = (bf16[1,1,5120]{2,0,1:T(2,128)(2,1)S(1)}, bf16[1,1,5120]{2,0,1:T(2,128)(2,1)S(1)}, u32[]{:S(2)}, u32[]{:S(2)}) collective-permute-start(bf16[1,1,5120]{2,0,1:T(2,128)(2,1)S(1)} %get-tuple-element.593), channel_id=1, source_target_pairs={{0,14},{1,15},{2,12},{3,13},{4,10},{5,11},{6,8},{7,9},{8,6},{9,7},... | collective-permute-start | bytes 30728 | tf_op jit(solution)/shard_map/while/body/eval_jaxpr/ppermute | solution.py:23
  99.3 2.5 %collective-permute-start.15 = (bf16[1,1,5120]{2,0,1:T(2,128)(2,1)S(1)}, bf16[1,1,5120]{2,0,1:T(2,128)(2,1)S(1)}, u32[]{:S(2)}, u32[]{:S(2)}) collective-permute-start(bf16[1,1,5120]{2,0,1:T(2,128)(2,1)S(1)} %get-tuple-element.594), channel_id=1, source_target_pairs={{0,15},{1,14},{2,13},{3,12},{4,11},{5,10},{6,9},{7,8},{8,7},{9,6},... | collective-permute-start | bytes 30728 | tf_op jit(solution)/shard_map/while/body/eval_jaxpr/ppermute | solution.py:23
  106.6 3.0 %fusion.61 = bf16[16,1,5120]{2,0,1:T(8,128)(2,1)S(1)} fusion(bf16[1,192,5120]{2,1,0:T(8,128)(2,1)} %get-tuple-element.670, bf16[16,5120]{1,0:T(8,128)(2,1)S(1)} %dynamic_update_slice.259, bf16[1,192,5120]{2,1,0:T(8,128)(2,1)S(1)} %copy-done.1), kind=kOutput, calls=%fused_computation.3.clone.1 | convolution fusion | flops 63011840 | bytes 4259840 | tf_op jit(solution)/shard_map/while/body/eval_jaxpr/dot_general | solution.py:64
  110.1 0.6 reduce.11
  110.8 0.8 reshape.326
  111.5 3.5 %all-to-all-start = ((bf16[16,2,2560]{2,1,0:T(2,128)(2,1)}), bf16[16,2,2560]{2,1,0:T(2,128)(2,1)S(1)}, u32[]{:S(2)}, u32[]{:S(2)}) async-start(bf16[16,2,2560]{2,1,0:T(2,128)(2,1)} %reshape.326), calls=%async_computation | async-start | bytes 327680 | tf_op jit(solution)/shard_map/while/body/eval_jaxpr/all_to_all | solution.py:85
  115.3 8.1 %all-to-all-done = bf16[16,2,2560]{2,1,0:T(2,128)(2,1)S(1)} async-done(((bf16[16,2,2560]{2,1,0:T(2,128)(2,1)}), bf16[16,2,2560]{2,1,0:T(2,128)(2,1)S(1)}, u32[]{:S(2)}, u32[]{:S(2)}) %all-to-all-start) | async-done | bytes 163872 | tf_op jit(solution)/shard_map/while/body/eval_jaxpr/all_to_all | solution.py:85
  124.1 0.9 bitcast_select_fusion.4
  125.0 0.7 copy-done.3
  125.7 0.8 broadcast_select_fusion.1
  126.5 24.3 %all-reduce.2.cloned.1.call-done = bf16[1,32,5120]{2,1,0:T(8,128)(2,1)} async-done(((bf16[1,32,5120]{2,1,0:T(8,128)(2,1)}), bf16[1,32,5120]{2,1,0:T(8,128)(2,1)}) %all-reduce.2.cloned.1.call-update) | async-done | bytes 327696 | tf_op jit(solution)/shard_map/psum | solution.py:36
  150.7 1.1 fusion.23
  151.9 1.9 %fusion.22 = bf16[1,1,32,64]{3,2,1,0:T(8,128)(2,1)} fusion(bf16[1,64,5120]{2,1,0:T(8,128)(2,1)S(1)} %copy-done, bf16[1,32,5120]{2,1,0:T(8,128)(2,1)} %all-reduce.2.cloned.1.call-done, f32[32]{0:T(128)S(1)} %add_rsqrt_fusion.1), kind=kOutput, calls=%fused_computation.47 | convolution fusion | flops 21465088 | bytes 987264 | tf_op jit(solution)/shard_map/mtd,jd->mtj/dot_general | solution.py:116
  (119 shorter events, 14.9 us)
Async XLA Ops:
  6.5 145.4 %copy-start = (bf16[1,64,5120]{2,1,0:T(8,128)(2,1)S(1)}, bf16[1,64,5120]{2,1,0:T(8,128)(2,1)}, u32[]{:S(2)}) copy-start(bf16[1,64,5120]{2,1,0:T(8,128)(2,1)} %param.13) | copy-start | bytes 1966084
  6.5 144.2 %all-reduce.2.cloned.1.call-start = ((), (), s32[]{:S(2)}) async-start(), calls=%async_computation.1 | async-start | bytes 655360 | tf_op jit(solution)/shard_map/psum | solution.py:36
  7.7 40.7 %copy-start.1 = (bf16[1,192,5120]{2,1,0:T(8,128)(2,1)S(1)}, bf16[1,192,5120]{2,1,0:T(8,128)(2,1)}, u32[]{:S(2)}) copy-start(bf16[1,192,5120]{2,1,0:T(8,128)(2,1)} %get-tuple-element.669) | copy-start | bytes 5898244 | tf_op jit(solution)/shard_map/while
  7.7 12.0 %collective-permute-start = (bf16[32,5120]{1,0:T(8,128)(2,1)S(1)}, bf16[32,5120]{1,0:T(8,128)(2,1)S(1)}, u32[]{:S(2)}, u32[]{:S(2)}) collective-permute-start(bf16[32,5120]{1,0:T(8,128)(2,1)S(1)} %broadcast_select_fusion.3), channel_id=1, source_target_pairs={{0,16},{1,17},{2,18},{3,19},{4,20},{5,21},{6,22},{7,23},{8,24},{9,... | collective-permute-start | bytes 983048 | tf_op jit(solution)/shard_map/while/body/eval_jaxpr/ppermute | solution.py:31
  21.6 3.6 %collective-permute-start.1 = (bf16[1,1,5120]{2,0,1:T(2,128)(2,1)S(1)}, bf16[1,1,5120]{2,0,1:T(2,128)(2,1)S(1)}, u32[]{:S(2)}, u32[]{:S(2)}) collective-permute-start(bf16[1,1,5120]{2,0,1:T(2,128)(2,1)S(1)} %get-tuple-element.580), channel_id=1, source_target_pairs={{0,1},{1,0},{2,3},{3,2},{4,5},{5,4},{6,7},{7,6},{8,9},{9,8},{10,11... | collective-permute-start | bytes 30728 | tf_op jit(solution)/shard_map/while/body/eval_jaxpr/ppermute | solution.py:23
  21.6 6.1 %collective-permute-start.2 = (bf16[1,1,5120]{2,0,1:T(2,128)(2,1)S(1)}, bf16[1,1,5120]{2,0,1:T(2,128)(2,1)S(1)}, u32[]{:S(2)}, u32[]{:S(2)}) collective-permute-start(bf16[1,1,5120]{2,0,1:T(2,128)(2,1)S(1)} %get-tuple-element.581), channel_id=1, source_target_pairs={{0,2},{1,3},{2,0},{3,1},{4,6},{5,7},{6,4},{7,5},{8,10},{9,11},{10,... | collective-permute-start | bytes 30728 | tf_op jit(solution)/shard_map/while/body/eval_jaxpr/ppermute | solution.py:23
  23.2 4.7 %collective-permute-start.3 = (bf16[1,1,5120]{2,0,1:T(2,128)(2,1)S(1)}, bf16[1,1,5120]{2,0,1:T(2,128)(2,1)S(1)}, u32[]{:S(2)}, u32[]{:S(2)}) collective-permute-start(bf16[1,1,5120]{2,0,1:T(2,128)(2,1)S(1)} %get-tuple-element.582), channel_id=1, source_target_pairs={{0,3},{1,2},{2,1},{3,0},{4,7},{5,6},{6,5},{7,4},{8,11},{9,10},{10,... | collective-permute-start | bytes 30728 | tf_op jit(solution)/shard_map/while/body/eval_jaxpr/ppermute | solution.py:23
  23.5 7.0 %collective-permute-start.4 = (bf16[1,1,5120]{2,0,1:T(2,128)(2,1)S(1)}, bf16[1,1,5120]{2,0,1:T(2,128)(2,1)S(1)}, u32[]{:S(2)}, u32[]{:S(2)}) collective-permute-start(bf16[1,1,5120]{2,0,1:T(2,128)(2,1)S(1)} %get-tuple-element.583), channel_id=1, source_target_pairs={{0,4},{1,5},{2,6},{3,7},{4,0},{5,1},{6,2},{7,3},{8,12},{9,13},{10,... | collective-permute-start | bytes 30728 | tf_op jit(solution)/shard_map/while/body/eval_jaxpr/ppermute | solution.py:23
  25.1 5.5 %collective-permute-start.5 = (bf16[1,1,5120]{2,0,1:T(2,128)(2,1)S(1)}, bf16[1,1,5120]{2,0,1:T(2,128)(2,1)S(1)}, u32[]{:S(2)}, u32[]{:S(2)}) collective-permute-start(bf16[1,1,5120]{2,0,1:T(2,128)(2,1)S(1)} %get-tuple-element.584), channel_id=1, source_target_pairs={{0,5},{1,4},{2,7},{3,6},{4,1},{5,0},{6,3},{7,2},{8,13},{9,12},{10,... | collective-permute-start | bytes 30728 | tf_op jit(solution)/shard_map/while/body/eval_jaxpr/ppermute | solution.py:23
  25.2 8.9 %collective-permute-start.6 = (bf16[1,1,5120]{2,0,1:T(2,128)(2,1)S(1)}, bf16[1,1,5120]{2,0,1:T(2,128)(2,1)S(1)}, u32[]{:S(2)}, u32[]{:S(2)}) collective-permute-start(bf16[1,1,5120]{2,0,1:T(2,128)(2,1)S(1)} %get-tuple-element.585), channel_id=1, source_target_pairs={{0,6},{1,7},{2,4},{3,5},{4,2},{5,3},{6,0},{7,1},{8,14},{9,15},{10,... | collective-permute-start | bytes 30728 | tf_op jit(solution)/shard_map/while/body/eval_jaxpr/ppermute | solution.py:23
  27.7 6.4 %collective-permute-start.7 = (bf16[1,1,5120]{2,0,1:T(2,128)(2,1)S(1)}, bf16[1,1,5120]{2,0,1:T(2,128)(2,1)S(1)}, u32[]{:S(2)}, u32[]{:S(2)}) collective-permute-start(bf16[1,1,5120]{2,0,1:T(2,128)(2,1)S(1)} %get-tuple-element.586), channel_id=1, source_target_pairs={{0,7},{1,6},{2,5},{3,4},{4,3},{5,2},{6,1},{7,0},{8,15},{9,14},{10,... | collective-permute-start | bytes 30728 | tf_op jit(solution)/shard_map/while/body/eval_jaxpr/ppermute | solution.py:23
  27.9 9.8 %collective-permute-start.8 = (bf16[1,1,5120]{2,0,1:T(2,128)(2,1)S(1)}, bf16[1,1,5120]{2,0,1:T(2,128)(2,1)S(1)}, u32[]{:S(2)}, u32[]{:S(2)}) collective-permute-start(bf16[1,1,5120]{2,0,1:T(2,128)(2,1)S(1)} %get-tuple-element.587), channel_id=1, source_target_pairs={{0,8},{1,9},{2,10},{3,11},{4,12},{5,13},{6,14},{7,15},{8,0},{9,1},... | collective-permute-start | bytes 30728 | tf_op jit(solution)/shard_map/while/body/eval_jaxpr/ppermute | solution.py:23
  30.5 7.3 %collective-permute-start.9 = (bf16[1,1,5120]{2,0,1:T(2,128)(2,1)S(1)}, bf16[1,1,5120]{2,0,1:T(2,128)(2,1)S(1)}, u32[]{:S(2)}, u32[]{:S(2)}) collective-permute-start(bf16[1,1,5120]{2,0,1:T(2,128)(2,1)S(1)} %get-tuple-element.588), channel_id=1, source_target_pairs={{0,9},{1,8},{2,11},{3,10},{4,13},{5,12},{6,15},{7,14},{8,1},{9,0},... | collective-permute-start | bytes 30728 | tf_op jit(solution)/shard_map/while/body/eval_jaxpr/ppermute | solution.py:23
  30.6 11.6 %collective-permute-start.10 = (bf16[1,1,5120]{2,0,1:T(2,128)(2,1)S(1)}, bf16[1,1,5120]{2,0,1:T(2,128)(2,1)S(1)}, u32[]{:S(2)}, u32[]{:S(2)}) collective-permute-start(bf16[1,1,5120]{2,0,1:T(2,128)(2,1)S(1)} %get-tuple-element.589), channel_id=1, source_target_pairs={{0,10},{1,11},{2,8},{3,9},{4,14},{5,15},{6,12},{7,13},{8,2},{9,3},... | collective-permute-start | bytes 30728 | tf_op jit(solution)/shard_map/while/body/eval_jaxpr/ppermute | solution.py:23
  34.1 11.5 %collective-permute-start.11 = (bf16[1,1,5120]{2,0,1:T(2,128)(2,1)S(1)}, bf16[1,1,5120]{2,0,1:T(2,128)(2,1)S(1)}, u32[]{:S(2)}, u32[]{:S(2)}) collective-permute-start(bf16[1,1,5120]{2,0,1:T(2,128)(2,1)S(1)} %get-tuple-element.590), channel_id=1, source_target_pairs={{0,11},{1,10},{2,9},{3,8},{4,15},{5,14},{6,13},{7,12},{8,3},{9,2},... | collective-permute-start | bytes 30728 | tf_op jit(solution)/shard_map/while/body/eval_jaxpr/ppermute | solution.py:23
  34.2 11.7 %collective-permute-start.12 = (bf16[1,1,5120]{2,0,1:T(2,128)(2,1)S(1)}, bf16[1,1,5120]{2,0,1:T(2,128)(2,1)S(1)}, u32[]{:S(2)}, u32[]{:S(2)}) collective-permute-start(bf16[1,1,5120]{2,0,1:T(2,128)(2,1)S(1)} %get-tuple-element.591), channel_id=1, source_target_pairs={{0,12},{1,13},{2,14},{3,15},{4,8},{5,9},{6,10},{7,11},{8,4},{9,5},... | collective-permute-start | bytes 30728 | tf_op jit(solution)/shard_map/while/body/eval_jaxpr/ppermute | solution.py:23
  37.7 8.5 %collective-permute-start.13 = (bf16[1,1,5120]{2,0,1:T(2,128)(2,1)S(1)}, bf16[1,1,5120]{2,0,1:T(2,128)(2,1)S(1)}, u32[]{:S(2)}, u32[]{:S(2)}) collective-permute-start(bf16[1,1,5120]{2,0,1:T(2,128)(2,1)S(1)} %get-tuple-element.592), channel_id=1, source_target_pairs={{0,13},{1,12},{2,15},{3,14},{4,9},{5,8},{6,11},{7,10},{8,5},{9,4},... | collective-permute-start | bytes 30728 | tf_op jit(solution)/shard_map/while/body/eval_jaxpr/ppermute | solution.py:23
  37.7 8.7 %collective-permute-start.14 = (bf16[1,1,5120]{2,0,1:T(2,128)(2,1)S(1)}, bf16[1,1,5120]{2,0,1:T(2,128)(2,1)S(1)}, u32[]{:S(2)}, u32[]{:S(2)}) collective-permute-start(bf16[1,1,5120]{2,0,1:T(2,128)(2,1)S(1)} %get-tuple-element.593), channel_id=1, source_target_pairs={{0,14},{1,15},{2,12},{3,13},{4,10},{5,11},{6,8},{7,9},{8,6},{9,7},... | collective-permute-start | bytes 30728 | tf_op jit(solution)/shard_map/while/body/eval_jaxpr/ppermute | solution.py:23
  42.2 5.9 %collective-permute-start.15 = (bf16[1,1,5120]{2,0,1:T(2,128)(2,1)S(1)}, bf16[1,1,5120]{2,0,1:T(2,128)(2,1)S(1)}, u32[]{:S(2)}, u32[]{:S(2)}) collective-permute-start(bf16[1,1,5120]{2,0,1:T(2,128)(2,1)S(1)} %get-tuple-element.594), channel_id=1, source_target_pairs={{0,15},{1,14},{2,13},{3,12},{4,11},{5,10},{6,9},{7,8},{8,7},{9,6},... | collective-permute-start | bytes 30728 | tf_op jit(solution)/shard_map/while/body/eval_jaxpr/ppermute | solution.py:23
  48.3 9.5 %copy-start.4 = (bf16[1,5120,2]{1,2,0:T(2,128)(2,1)S(1)}, bf16[1,5120,2]{1,2,0:T(2,128)(2,1)}, u32[]{:S(2)}) copy-start(bf16[1,5120,2]{1,2,0:T(2,128)(2,1)} %get-tuple-element.666) | copy-start | bytes 61444 | tf_op jit(solution)/shard_map/while
  51.4 15.4 %copy-start.2 = (bf16[1,32,5120]{2,1,0:T(8,128)(2,1)S(1)}, bf16[1,32,5120]{2,1,0:T(8,128)(2,1)}, u32[]{:S(2)}) copy-start(bf16[1,32,5120]{2,1,0:T(8,128)(2,1)} %get-tuple-element.631) | copy-start | bytes 983044 | tf_op jit(solution)/shard_map/while
  53.3 12.9 %all-to-all-start = ((bf16[16,2,2560]{2,1,0:T(2,128)(2,1)}), bf16[16,2,2560]{2,1,0:T(2,128)(2,1)S(1)}, u32[]{:S(2)}, u32[]{:S(2)}) async-start(bf16[16,2,2560]{2,1,0:T(2,128)(2,1)} %reshape.326), calls=%async_computation | async-start | bytes 327680 | tf_op jit(solution)/shard_map/while/body/eval_jaxpr/all_to_all | solution.py:85
  67.7 0.7 copy-start.3
  68.4 38.1 %copy-start.1 = (bf16[1,192,5120]{2,1,0:T(8,128)(2,1)S(1)}, bf16[1,192,5120]{2,1,0:T(8,128)(2,1)}, u32[]{:S(2)}) copy-start(bf16[1,192,5120]{2,1,0:T(8,128)(2,1)} %get-tuple-element.669) | copy-start | bytes 5898244 | tf_op jit(solution)/shard_map/while
  68.5 10.9 %collective-permute-start = (bf16[32,5120]{1,0:T(8,128)(2,1)S(1)}, bf16[32,5120]{1,0:T(8,128)(2,1)S(1)}, u32[]{:S(2)}, u32[]{:S(2)}) collective-permute-start(bf16[32,5120]{1,0:T(8,128)(2,1)S(1)} %broadcast_select_fusion.3), channel_id=1, source_target_pairs={{0,16},{1,17},{2,18},{3,19},{4,20},{5,21},{6,22},{7,23},{8,24},{9,... | collective-permute-start | bytes 983048 | tf_op jit(solution)/shard_map/while/body/eval_jaxpr/ppermute | solution.py:31
  81.2 3.6 %collective-permute-start.1 = (bf16[1,1,5120]{2,0,1:T(2,128)(2,1)S(1)}, bf16[1,1,5120]{2,0,1:T(2,128)(2,1)S(1)}, u32[]{:S(2)}, u32[]{:S(2)}) collective-permute-start(bf16[1,1,5120]{2,0,1:T(2,128)(2,1)S(1)} %get-tuple-element.580), channel_id=1, source_target_pairs={{0,1},{1,0},{2,3},{3,2},{4,5},{5,4},{6,7},{7,6},{8,9},{9,8},{10,11... | collective-permute-start | bytes 30728 | tf_op jit(solution)/shard_map/while/body/eval_jaxpr/ppermute | solution.py:23
  81.3 4.7 %collective-permute-start.2 = (bf16[1,1,5120]{2,0,1:T(2,128)(2,1)S(1)}, bf16[1,1,5120]{2,0,1:T(2,128)(2,1)S(1)}, u32[]{:S(2)}, u32[]{:S(2)}) collective-permute-start(bf16[1,1,5120]{2,0,1:T(2,128)(2,1)S(1)} %get-tuple-element.581), channel_id=1, source_target_pairs={{0,2},{1,3},{2,0},{3,1},{4,6},{5,7},{6,4},{7,5},{8,10},{9,11},{10,... | collective-permute-start | bytes 30728 | tf_op jit(solution)/shard_map/while/body/eval_jaxpr/ppermute | solution.py:23
  82.1 5.5 %collective-permute-start.3 = (bf16[1,1,5120]{2,0,1:T(2,128)(2,1)S(1)}, bf16[1,1,5120]{2,0,1:T(2,128)(2,1)S(1)}, u32[]{:S(2)}, u32[]{:S(2)}) collective-permute-start(bf16[1,1,5120]{2,0,1:T(2,128)(2,1)S(1)} %get-tuple-element.582), channel_id=1, source_target_pairs={{0,3},{1,2},{2,1},{3,0},{4,7},{5,6},{6,5},{7,4},{8,11},{9,10},{10,... | collective-permute-start | bytes 30728 | tf_op jit(solution)/shard_map/while/body/eval_jaxpr/ppermute | solution.py:23
  83.2 5.4 %collective-permute-start.4 = (bf16[1,1,5120]{2,0,1:T(2,128)(2,1)S(1)}, bf16[1,1,5120]{2,0,1:T(2,128)(2,1)S(1)}, u32[]{:S(2)}, u32[]{:S(2)}) collective-permute-start(bf16[1,1,5120]{2,0,1:T(2,128)(2,1)S(1)} %get-tuple-element.583), channel_id=1, source_target_pairs={{0,4},{1,5},{2,6},{3,7},{4,0},{5,1},{6,2},{7,3},{8,12},{9,13},{10,... | collective-permute-start | bytes 30728 | tf_op jit(solution)/shard_map/while/body/eval_jaxpr/ppermute | solution.py:23
  84.1 6.1 %collective-permute-start.5 = (bf16[1,1,5120]{2,0,1:T(2,128)(2,1)S(1)}, bf16[1,1,5120]{2,0,1:T(2,128)(2,1)S(1)}, u32[]{:S(2)}, u32[]{:S(2)}) collective-permute-start(bf16[1,1,5120]{2,0,1:T(2,128)(2,1)S(1)} %get-tuple-element.584), channel_id=1, source_target_pairs={{0,5},{1,4},{2,7},{3,6},{4,1},{5,0},{6,3},{7,2},{8,13},{9,12},{10,... | collective-permute-start | bytes 30728 | tf_op jit(solution)/shard_map/while/body/eval_jaxpr/ppermute | solution.py:23
  84.9 6.4 %collective-permute-start.6 = (bf16[1,1,5120]{2,0,1:T(2,128)(2,1)S(1)}, bf16[1,1,5120]{2,0,1:T(2,128)(2,1)S(1)}, u32[]{:S(2)}, u32[]{:S(2)}) collective-permute-start(bf16[1,1,5120]{2,0,1:T(2,128)(2,1)S(1)} %get-tuple-element.585), channel_id=1, source_target_pairs={{0,6},{1,7},{2,4},{3,5},{4,2},{5,3},{6,0},{7,1},{8,14},{9,15},{10,... | collective-permute-start | bytes 30728 | tf_op jit(solution)/shard_map/while/body/eval_jaxpr/ppermute | solution.py:23
  86.0 7.8 %collective-permute-start.7 = (bf16[1,1,5120]{2,0,1:T(2,128)(2,1)S(1)}, bf16[1,1,5120]{2,0,1:T(2,128)(2,1)S(1)}, u32[]{:S(2)}, u32[]{:S(2)}) collective-permute-start(bf16[1,1,5120]{2,0,1:T(2,128)(2,1)S(1)} %get-tuple-element.586), channel_id=1, source_target_pairs={{0,7},{1,6},{2,5},{3,4},{4,3},{5,2},{6,1},{7,0},{8,15},{9,14},{10,... | collective-permute-start | bytes 30728 | tf_op jit(solution)/shard_map/while/body/eval_jaxpr/ppermute | solution.py:23
  87.6 8.0 %collective-permute-start.8 = (bf16[1,1,5120]{2,0,1:T(2,128)(2,1)S(1)}, bf16[1,1,5120]{2,0,1:T(2,128)(2,1)S(1)}, u32[]{:S(2)}, u32[]{:S(2)}) collective-permute-start(bf16[1,1,5120]{2,0,1:T(2,128)(2,1)S(1)} %get-tuple-element.587), channel_id=1, source_target_pairs={{0,8},{1,9},{2,10},{3,11},{4,12},{5,13},{6,14},{7,15},{8,0},{9,1},... | collective-permute-start | bytes 30728 | tf_op jit(solution)/shard_map/while/body/eval_jaxpr/ppermute | solution.py:23
  88.5 8.8 %collective-permute-start.9 = (bf16[1,1,5120]{2,0,1:T(2,128)(2,1)S(1)}, bf16[1,1,5120]{2,0,1:T(2,128)(2,1)S(1)}, u32[]{:S(2)}, u32[]{:S(2)}) collective-permute-start(bf16[1,1,5120]{2,0,1:T(2,128)(2,1)S(1)} %get-tuple-element.588), channel_id=1, source_target_pairs={{0,9},{1,8},{2,11},{3,10},{4,13},{5,12},{6,15},{7,14},{8,1},{9,0},... | collective-permute-start | bytes 30728 | tf_op jit(solution)/shard_map/while/body/eval_jaxpr/ppermute | solution.py:23
  90.2 9.1 %collective-permute-start.10 = (bf16[1,1,5120]{2,0,1:T(2,128)(2,1)S(1)}, bf16[1,1,5120]{2,0,1:T(2,128)(2,1)S(1)}, u32[]{:S(2)}, u32[]{:S(2)}) collective-permute-start(bf16[1,1,5120]{2,0,1:T(2,128)(2,1)S(1)} %get-tuple-element.589), channel_id=1, source_target_pairs={{0,10},{1,11},{2,8},{3,9},{4,14},{5,15},{6,12},{7,13},{8,2},{9,3},... | collective-permute-start | bytes 30728 | tf_op jit(solution)/shard_map/while/body/eval_jaxpr/ppermute | solution.py:23
  91.3 13.7 %collective-permute-start.11 = (bf16[1,1,5120]{2,0,1:T(2,128)(2,1)S(1)}, bf16[1,1,5120]{2,0,1:T(2,128)(2,1)S(1)}, u32[]{:S(2)}, u32[]{:S(2)}) collective-permute-start(bf16[1,1,5120]{2,0,1:T(2,128)(2,1)S(1)} %get-tuple-element.590), channel_id=1, source_target_pairs={{0,11},{1,10},{2,9},{3,8},{4,15},{5,14},{6,13},{7,12},{8,3},{9,2},... | collective-permute-start | bytes 30728 | tf_op jit(solution)/shard_map/while/body/eval_jaxpr/ppermute | solution.py:23
  93.8 11.6 %collective-permute-start.12 = (bf16[1,1,5120]{2,0,1:T(2,128)(2,1)S(1)}, bf16[1,1,5120]{2,0,1:T(2,128)(2,1)S(1)}, u32[]{:S(2)}, u32[]{:S(2)}) collective-permute-start(bf16[1,1,5120]{2,0,1:T(2,128)(2,1)S(1)} %get-tuple-element.591), channel_id=1, source_target_pairs={{0,12},{1,13},{2,14},{3,15},{4,8},{5,9},{6,10},{7,11},{8,4},{9,5},... | collective-permute-start | bytes 30728 | tf_op jit(solution)/shard_map/while/body/eval_jaxpr/ppermute | solution.py:23
  95.6 10.1 %collective-permute-start.13 = (bf16[1,1,5120]{2,0,1:T(2,128)(2,1)S(1)}, bf16[1,1,5120]{2,0,1:T(2,128)(2,1)S(1)}, u32[]{:S(2)}, u32[]{:S(2)}) collective-permute-start(bf16[1,1,5120]{2,0,1:T(2,128)(2,1)S(1)} %get-tuple-element.592), channel_id=1, source_target_pairs={{0,13},{1,12},{2,15},{3,14},{4,9},{5,8},{6,11},{7,10},{8,5},{9,4},... | collective-permute-start | bytes 30728 | tf_op jit(solution)/shard_map/while/body/eval_jaxpr/ppermute | solution.py:23
  97.3 8.7 %collective-permute-start.14 = (bf16[1,1,5120]{2,0,1:T(2,128)(2,1)S(1)}, bf16[1,1,5120]{2,0,1:T(2,128)(2,1)S(1)}, u32[]{:S(2)}, u32[]{:S(2)}) collective-permute-start(bf16[1,1,5120]{2,0,1:T(2,128)(2,1)S(1)} %get-tuple-element.593), channel_id=1, source_target_pairs={{0,14},{1,15},{2,12},{3,13},{4,10},{5,11},{6,8},{7,9},{8,6},{9,7},... | collective-permute-start | bytes 30728 | tf_op jit(solution)/shard_map/while/body/eval_jaxpr/ppermute | solution.py:23
  99.3 7.0 %collective-permute-start.15 = (bf16[1,1,5120]{2,0,1:T(2,128)(2,1)S(1)}, bf16[1,1,5120]{2,0,1:T(2,128)(2,1)S(1)}, u32[]{:S(2)}, u32[]{:S(2)}) collective-permute-start(bf16[1,1,5120]{2,0,1:T(2,128)(2,1)S(1)} %get-tuple-element.594), channel_id=1, source_target_pairs={{0,15},{1,14},{2,13},{3,12},{4,11},{5,10},{6,9},{7,8},{8,7},{9,6},... | collective-permute-start | bytes 30728 | tf_op jit(solution)/shard_map/while/body/eval_jaxpr/ppermute | solution.py:23
  106.6 8.5 %copy-start.4 = (bf16[1,5120,2]{1,2,0:T(2,128)(2,1)S(1)}, bf16[1,5120,2]{1,2,0:T(2,128)(2,1)}, u32[]{:S(2)}) copy-start(bf16[1,5120,2]{1,2,0:T(2,128)(2,1)} %get-tuple-element.666) | copy-start | bytes 61444 | tf_op jit(solution)/shard_map/while
  109.6 14.4 %copy-start.2 = (bf16[1,32,5120]{2,1,0:T(8,128)(2,1)S(1)}, bf16[1,32,5120]{2,1,0:T(8,128)(2,1)}, u32[]{:S(2)}) copy-start(bf16[1,32,5120]{2,1,0:T(8,128)(2,1)} %get-tuple-element.631) | copy-start | bytes 983044 | tf_op jit(solution)/shard_map/while
  111.5 11.9 %all-to-all-start = ((bf16[16,2,2560]{2,1,0:T(2,128)(2,1)}), bf16[16,2,2560]{2,1,0:T(2,128)(2,1)S(1)}, u32[]{:S(2)}, u32[]{:S(2)}) async-start(bf16[16,2,2560]{2,1,0:T(2,128)(2,1)} %reshape.326), calls=%async_computation | async-start | bytes 327680 | tf_op jit(solution)/shard_map/while/body/eval_jaxpr/all_to_all | solution.py:85
  124.9 0.7 copy-start.3
Sparse Core Ops, SparseCore 0:
  126.6 24.1 all-reduce.1
